TPU v7x, 512 devices: a whole 4x4x16 slice. The times are simulated.
512 devices in a mesh: walk: 32 (over z, core), chol: 16 (over y, x).
Axes of the slice: x: 4, y: 4, z: 16, core: 2. Of those that a mesh axis runs over, the one named last changes fastest.
Arguments:
- walkers: float32 [64, 512, 200], P('walk'), as said below
- cholesky: float32 [32, 512, 512], P('chol'), as said below
- fields: float32 [64, 32], P('walk', 'chol'), may hold values from -4 to 4
- weights: float32 [64], P('walk'), may hold values from 0.5 to 2
- counts: int32 [64], P('walk'), may hold values from 0 to 4, as said below
Outputs:
- routed: float32 [64, 512, 200], P('walk')
- comb_marks: float32 [64], P('walk')
Inputs may be any that keep to these rules, and one draw needn't show every extreme that they name: The counts sum to 64. Some walker has 4 copies in every draw. `walkers`: for every walker the intersection matrix (its first 100 rows) differs from the identity by a matrix of spectral norm below one. `cholesky`: each vector is a symmetric matrix.
All inputs are finite; a program needn't handle non-finite values.
Results may differ from a plain program's by a relative error of at most 0.0001.
Values sent between devices are 32-bit elements; how exact they have to be, the bound alone decides.
A program may use at most 64 MiB of HBM per device.

v0:
```python
import jax
import jax.numpy as jnp
from jax import lax
from jax.sharding import PartitionSpec as P

TAYLOR = 3
NEWTON = 3


highest = lax.Precision.HIGHEST
root_dt = 0.1


def entering(part, axis, combine, identity):
    place = lax.axis_index(axis)
    gathered = jax.tree.map(lambda a: lax.all_gather(a, axis), part)
    state = jax.tree.map(lambda a, e: jnp.zeros_like(a) + jnp.asarray(e, a.dtype), part, identity)

    def one(step, state):
        return combine(
            state, jax.tree.map(lambda a: lax.dynamic_index_in_dim(a, step, 0, False), gathered)
        )

    return lax.fori_loop(0, place, one, state)


def from_behind(block, axis, distance):
    devices = range(lax.axis_size(axis))
    route = [(i - distance, i) for i in devices if i - distance in devices]
    return lax.ppermute(block, axis, route)


def rotate(block):
    half_width = block.shape[-1] // 2
    return jnp.concatenate([-block[..., half_width:], block[..., :half_width]], axis=-1)


def batch_product(left, right):
    return jnp.einsum("wab,wbc->wac", left, right, precision=highest)


def complex_batch(left_real, left_imag, right_real, right_imag):
    real_part = batch_product(left_real, right_real) - batch_product(left_imag, right_imag)
    imag_part = batch_product(left_real, right_imag) + batch_product(left_imag, right_real)
    return (real_part, imag_part)


def intersection_inverse(over_real, over_imag):
    identity = jnp.broadcast_to(jnp.eye(over_real.shape[1], dtype=jnp.float32), over_real.shape)
    inv_real = identity
    inv_imag = jnp.zeros_like(identity)
    for sweep_step in range(NEWTON):
        prod_real, prod_imag = complex_batch(over_real, over_imag, inv_real, inv_imag)
        inv_real, inv_imag = complex_batch(
            inv_real, inv_imag, 2.0 * identity - prod_real, -prod_imag
        )
    return (inv_real, inv_imag)


def add_pair(earlier, later):
    return (earlier[0] + later[0], earlier[1] + later[1])


def on_device(walkers, cholesky, fields, weights, counts):
    count_walk = walkers.shape[0]
    electrons = walkers.shape[2] // 2
    walk_real = walkers[:, :, :electrons]
    walk_imag = walkers[:, :, electrons:]
    inv_real, inv_imag = intersection_inverse(walk_real[:, :electrons], walk_imag[:, :electrons])
    theta_real, theta_imag = complex_batch(walk_real, walk_imag, inv_real, inv_imag)
    top_rows = cholesky[:, :electrons, :]
    force_real = root_dt * jnp.einsum("gak,wka->wg", top_rows, theta_real, precision=highest)
    force_imag = root_dt * jnp.einsum("gak,wka->wg", top_rows, theta_imag, precision=highest)
    coeff_real = root_dt * force_imag
    coeff_imag = root_dt * (fields - force_real)
    log_part = jnp.sum(
        fields * force_real - 0.5 * (force_real * force_real - force_imag * force_imag), axis=1
    )
    log_weight = lax.psum(log_part, "chol")
    series = walkers
    taylor_term = walkers
    oper_real = jnp.einsum("wg,gik->wik", coeff_real, cholesky, precision=highest)
    oper_imag = jnp.einsum("wg,gik->wik", coeff_imag, cholesky, precision=highest)
    for degree in range(1, TAYLOR + 1):
        partial_value = (
            batch_product(oper_real, taylor_term) + batch_product(oper_imag, rotate(taylor_term))
        ) / degree
        taylor_term = lax.psum(partial_value, "chol")
        series = series + taylor_term
    new_weights = weights * jnp.exp(log_weight)
    group_weight = jnp.sum(new_weights)
    group_count = jnp.sum(counts)
    groups = lax.axis_size("walk")
    group_index = lax.axis_index("walk")
    base_weight, base_count = entering(
        (group_weight, group_count), "walk", add_pair, (jnp.float32(0.0), jnp.int32(0))
    )
    total_weight = lax.psum(group_weight, "walk")
    comb_marks = groups * count_walk * (base_weight + jnp.cumsum(new_weights)) / total_weight
    starts = (base_count + jnp.cumsum(counts) - counts).astype(jnp.int32)
    end_marks = starts + counts
    slot_ids = jnp.arange(count_walk, dtype=jnp.int32)

    def selection(offset):
        target = (group_index + offset) * count_walk + slot_ids
        inside = (starts[None, :] <= target[:, None]) & (target[:, None] < end_marks[None, :])
        return inside.astype(jnp.float32)

    def pick(offset, source):
        return jnp.einsum("rj,jne->rne", selection(offset), source, precision=highest)

    routed = pick(0, series)
    for offset in (1, -1):
        routed = routed + from_behind(pick(offset, series), "walk", offset)
    return (routed, comb_marks)


def solution(mesh):
    in_specs = (
        P("walk", None, None),
        P("chol", None, None),
        P("walk", "chol"),
        P("walk"),
        P("walk"),
    )
    out_specs = (P("walk", None, None), P("walk"))
    return jax.shard_map(
        on_device, mesh=mesh, in_specs=in_specs, out_specs=out_specs, check_vma=False
    )
```

profile of v0, /device:TPU:480, one launch (start us, length us, event | category | flops | bytes accessed | tf_op | source)
XLA Modules:
  0.0 526.2 jit_solution(10204763451858970211)
XLA Ops:
  7.3 1.3 fusion.74
  8.6 2.0 slice_negate_fusion.2
  18.8 1.4 fusion.135
  20.1 1.3 fusion.56
  21.8 1.3 fusion.58
  23.1 1.3 fusion.133
  24.4 1.6 copy.28
  26.2 1.2 copy-done.4
  27.4 5.0 fusion.37
  32.4 10.3 %fusion.104 = f32[2,512,512]{2,0,1:T(2,128)S(1)} fusion(f32[2,512,512]{2,0,1:T(2,128)} %copy-done.4, f32[2,2]{0,1:T(2,128)S(1)} %copy.29, f32[2,2]{0,1:T(2,128)S(1)} %fusion.37), kind=kOutput, calls=%fused_computation.116 | convolution fusion | flops 12582920 | bytes 4194336 | tf_op jit(solution)/shard_map/wg,gik->wik/dot_general | solution.py:83
  42.8 3.7 subtract_reduce_fusion
  46.5 9.3 %fusion.106 = f32[2,512,512]{2,0,1:T(2,128)S(1)} fusion(f32[2,512,512]{2,0,1:T(2,128)S(1)} %copy-done.5, f32[2,2]{0,1:T(2,128)S(1)} %get-tuple-element.65), kind=kOutput, calls=%fused_computation.118 | convolution fusion | flops 12582916 | bytes 4194320 | tf_op jit(solution)/shard_map/wg,gik->wik/dot_general | solution.py:82
  55.8 2.5 fusion.4
  58.3 3.4 fusion.12
  61.8 116.0 %all-reduce.7.cloned.1.call-done = f32[2,512,200]{1,2,0:T(8,128)} async-done(((f32[2,512,200]{1,2,0:T(8,128)}), f32[2,512,200]{1,2,0:T(8,128)}) %all-reduce.7.cloned.1.call-update) | async-done | bytes 819216 | tf_op jit(solution)/shard_map/psum | solution.py:88
  177.9 1.2 slice_negate_fusion.1
  179.1 2.5 fusion.2
  181.7 3.4 fusion.18
  185.3 116.0 %all-reduce.9.cloned.1.call-done = f32[2,512,200]{1,2,0:T(8,128)} async-done(((f32[2,512,200]{1,2,0:T(8,128)}), f32[2,512,200]{1,2,0:T(8,128)}) %all-reduce.9.cloned.1.call-update) | async-done | bytes 819216 | tf_op jit(solution)/shard_map/psum | solution.py:88
  301.4 1.2 slice_negate_fusion
  302.6 2.5 fusion
  305.2 3.4 fusion.24
  308.7 38.1 %psum.35 = f32[2]{0:T(128)S(1)} all-reduce(f32[2]{0:T(128)S(1)} %get-tuple-element.64), channel_id=1, replica_groups=mesh['walk'=32,'chol'=16] {'chol'}, use_global_device_ids=true, to_apply=%region_1.0 | all-reduce | flops 2 | bytes 16 | tf_op jit(solution)/shard_map/psum | solution.py:79
  346.8 0.7 reduce_sum.29
  347.7 1.3 dynamic-slice
  349.0 0.7 fusion.131
  349.6 1.4 dynamic-update-slice
  351.0 1.4 dynamic-update-slice.1
  352.4 43.1 %all-reduce.2 = (f32[32]{0:T(128)S(1)}, f32[]{:T(128)}) all-reduce(f32[32]{0:T(128)S(1)} %dynamic-update-slice, f32[]{:T(128)} %get-tuple-element.63), channel_id=1, replica_groups=mesh['walk'=32,'chol'=16] {'walk'}, use_global_device_ids=true, to_apply=%add | all-reduce | flops 33 | bytes 264
  395.6 20.9 %all-reduce.1 = s32[32]{0:T(128)S(1)} all-reduce(s32[32]{0:T(128)S(1)} %dynamic-update-slice.1), channel_id=1, replica_groups=mesh['walk'=32,'chol'=16] {'walk'}, use_global_device_ids=true, to_apply=%add.1 | all-reduce | flops 32 | bytes 256
  416.4 77.2 %while.12 = (s32[]{:T(128)}, f32[]{:T(128)}, s32[]{:T(128)}, s32[]{:T(128)}, f32[32]{0:T(128)S(1)}, /*index=5*/s32[32]{0:T(128)S(1)}, s32[]{:T(128)}, s32[]{:T(128)}, s32[]{:T(128)}) while((s32[]{:T(128)}, f32[]{:T(128)}, s32[]{:T(128)}, s32[]{:T(128)}, f32[32]{0:T(128)S(1)}, /*index=5*/s32[32]{0:T(128)S(1)}, s32[]{:T(128)}, s32[]{:T(128)}, ...), condition=%wide.region_5.0_spmd, body=%wide.region_4.0_spmd.sunk | while | flops 7 | bytes 183 | solution.py:24
  417.7 0.7 dynamic_slice.11
  420.3 0.7 dynamic_slice.11
  422.8 0.7 dynamic_slice.11
  425.4 0.7 dynamic_slice.11
  428.0 0.7 dynamic_slice.11
  430.6 0.7 dynamic_slice.11
  433.1 0.7 dynamic_slice.11
  493.7 1.5 add_add_fusion
  495.2 2.0 fusion.47
  497.2 1.9 collective-permute-start.1
  499.1 2.0 fusion.49
  501.1 2.7 collective-permute-start
  504.0 1.2 divide_bitcast_fusion
  505.2 3.8 collective-permute-done.1
  509.0 5.9 %collective-permute-done = f32[2,512,200]{1,0,2:T(2,128)} collective-permute-done((f32[2,512,200]{1,0,2:T(2,128)S(1)}, f32[2,512,200]{1,0,2:T(2,128)}, u32[]{:S(2)}, u32[]{:S(2)}) %collective-permute-start) | collective-permute-done | bytes 819232 | tf_op jit(solution)/shard_map/ppermute | solution.py:30
  514.9 3.5 fusion.27
  518.4 1.0 copy.44
  (128 shorter events, 43.7 us)
Async XLA Ops:
  7.2 3.5 copy-start
  7.2 170.7 %all-reduce.7.cloned.1.call-start = ((), (), s32[]{:S(2)}) async-start(), calls=%async_computation | async-start | bytes 1638400 | tf_op jit(solution)/shard_map/psum | solution.py:88
  18.8 5.6 %copy-start.10 = (f32[2,512,512]{2,1,0:T(8,128)S(1)}, f32[2,512,512]{2,1,0:T(8,128)}, u32[]{:S(2)}) copy-start(f32[2,512,512]{2,1,0:T(8,128)} %param.8) | copy-start | bytes 6291460
  24.4 1.6 copy-start.14
  26.1 1.3 copy-start.4
  32.4 10.3 %copy-start.5 = (f32[2,512,512]{2,0,1:T(2,128)S(1)}, f32[2,512,512]{2,0,1:T(2,128)}, u32[]{:S(2)}) copy-start(f32[2,512,512]{2,0,1:T(2,128)} %copy-done.4) | copy-start | bytes 6291460
  32.4 10.3 %copy-start.12 = (f32[2,100,512]{2,1,0:T(8,128)S(1)}, f32[2,100,512]{2,1,0:T(8,128)}, u32[]{:S(2)}) copy-start(f32[2,100,512]{2,1,0:T(8,128)} %fusion.56) | copy-start | bytes 1228804
  32.4 10.3 %copy-start.13 = (f32[2,100,512]{2,1,0:T(8,128)S(1)}, f32[2,100,512]{2,1,0:T(8,128)}, u32[]{:S(2)}) copy-start(f32[2,100,512]{2,1,0:T(8,128)} %fusion.133) | copy-start | bytes 1228804
  46.4 9.4 %copy-start.11 = (f32[2,512,100]{1,2,0:T(8,128)S(1)}, f32[2,512,100]{1,2,0:T(8,128)}, u32[]{:S(2)}) copy-start(f32[2,512,100]{1,2,0:T(8,128)} %get-tuple-element.61) | copy-start | bytes 1228804
  55.8 2.5 copy-start.1
  61.8 239.6 %all-reduce.9.cloned.1.call-start = ((), (), s32[]{:S(2)}) async-start(), calls=%async_computation.1 | async-start | bytes 1638400 | tf_op jit(solution)/shard_map/psum | solution.py:88
  179.1 2.6 copy-start.2
  179.1 2.6 copy-start.6
  185.1 308.5 %all-reduce.11.cloned.1.call-start = ((), (), s32[]{:S(2)}) async-start(), calls=%async_computation.2 | async-start | bytes 1638400 | tf_op jit(solution)/shard_map/psum | solution.py:88
  302.6 2.6 copy-start.3
  302.6 2.6 copy-start.8
  305.2 41.6 %copy-start.15 = (s32[2]{0:T(128)S(1)}, s32[2]{0:T(128)}, u32[]{:S(2)}) copy-start(s32[2]{0:T(128)} %param.11) | copy-start | bytes 28
  305.2 43.8 %copy-start.16 = (f32[2]{0:T(128)S(1)}, f32[2]{0:T(128)}, u32[]{:S(2)}) copy-start(f32[2]{0:T(128)} %param.10) | copy-start | bytes 28
  305.2 188.5 %copy-start.7 = (f32[2,512,200]{1,2,0:T(8,128)S(1)}, f32[2,512,200]{1,2,0:T(8,128)}, u32[]{:S(2)}) copy-start(f32[2,512,200]{1,2,0:T(8,128)} %all-reduce.7.cloned.1.call-done) | copy-start | bytes 2457604
  305.2 188.5 %copy-start.9 = (f32[2,512,200]{1,2,0:T(8,128)S(1)}, f32[2,512,200]{1,2,0:T(8,128)}, u32[]{:S(2)}) copy-start(f32[2,512,200]{1,2,0:T(8,128)} %all-reduce.9.cloned.1.call-done) | copy-start | bytes 2457604
  497.2 11.8 %collective-permute-start.1 = (f32[2,512,200]{1,0,2:T(2,128)S(1)}, f32[2,512,200]{1,0,2:T(2,128)S(1)}, u32[]{:S(2)}, u32[]{:S(2)}) collective-permute-start(f32[2,512,200]{1,0,2:T(2,128)S(1)} %fusion.47), channel_id=1, source_target_pairs={{16,0},{32,16},{48,32},{64,48},{80,64},{96,80},{112,96},{128,112},... | collective-permute-start | bytes 2457608 | tf_op jit(solution)/shard_map/ppermute | solution.py:30
  501.1 13.8 %collective-permute-start = (f32[2,512,200]{1,0,2:T(2,128)S(1)}, f32[2,512,200]{1,0,2:T(2,128)}, u32[]{:S(2)}, u32[]{:S(2)}) collective-permute-start(f32[2,512,200]{1,0,2:T(2,128)S(1)} %fusion.49), channel_id=1, source_target_pairs={{0,16},{16,32},{32,48},{48,64},{64,80},{80,96},{96,112},{112,128},... | collective-permute-start | bytes 2457608 | tf_op jit(solution)/shard_map/ppermute | solution.py:30
Sparse Core Ops, SparseCore 0:
  61.9 115.8 all-reduce.6
  185.2 116.0 all-reduce.8
  308.8 116.0 all-reduce.10
where the time goes:
time: 536 us; the launch traced here: 526 us
  waiting for transfers between devices  242 us (45%)
  blocking collectives  102 us (19%)
  matrix products  68.5 us (13%)
  local copies, waits for them, and re-layouts  47.2 us (9%)
  loops' own time  38.2 us (7%)
  between operations  14.5 us (3%)
  other arithmetic  8.9 us (2%)
    psum x3, waiting for transfers between devices, on_device(): taylor_term = lax.psum(partial_value, 'chol')  232 us
    unnamed x2, blocking collectives  64 us
    dynamic_slice x60, local copies, waits for them, and re-layouts, one(): lax.dynamic_index_in_dim(a, step, 0, False)  38.9 us
    another operation x1, loops' own time, entering(): return lax.fori_loop(0, place, one, state)  38.2 us
    psum x1, blocking collectives, on_device(): log_weight = lax.psum(log_part, 'chol')  38.1 us
    dot_general x34, matrix products, batch_product(): return jnp.einsum('wab,wbc->wac', left, right, precision=highest)  32.8 us
  transfers between devices with their start and end apart: 5, of which 4 were waited for; matrix products, arithmetic and copies ran while one was open for 9% of the time, Pallas kernels for 0%

commit v1 on v0

v1 whole, which is shorter than its diff:
```python
import functools

import jax
import jax.numpy as jnp
from jax import lax
from jax.experimental import pallas as pl
from jax.experimental.pallas import tpu as pltpu
from jax.sharding import PartitionSpec as P

F32 = jnp.float32
BF16 = jnp.bfloat16
MESH = pl.DeviceIdType.MESH
TAYLOR = 3
LANES = 128
ROOT_DT = 0.1


def split(a):
    high = a.astype(BF16)
    return high, (a - high.astype(F32)).astype(BF16)


def dot(a, b):
    return jnp.dot(a, b, preferred_element_type=F32)


def dot3(a, b):
    return dot(a[0], b[0]) + (dot(a[1], b[0]) + dot(a[0], b[1]))


def block_form(c):
    re, im = c[:, :LANES], c[:, LANES:]
    return jnp.concatenate([c, jnp.concatenate([-im, re], axis=1)], axis=0)


def kernel(
    nwalk, nchol, nelec,
    walk_hbm, chol_hbm, fields_s, weights_s, counts_s,
    out_ref, comb_s,
    wbuf, top, lrows, pall, phi, plo, msgs, q1, q2, ser, fin, near, ring,
    c_sem, l_send, l_recv, f_send, f_recv, m_send, m_recv,
    g_send, g_recv, r_send, r_recv, n_send, n_recv,
):
    w = lax.axis_index("walk")
    me = lax.axis_index("chol")
    core = lax.rem(w, 2)
    chip = lax.div(w, 2)
    nchip = nwalk // 2
    partner = w + 1 - 2 * core
    walks, norb = wbuf.shape[0], wbuf.shape[1]
    rows = norb // nchol
    depth = top.shape[1]

    def walk_id(shift):
        return {"walk": lax.rem(w + nwalk + shift, nwalk)}

    def block(owner):
        return pl.ds(pl.multiple_of(owner * rows, rows), rows)

    def remote(src, dst, send, recv, device):
        return pltpu.make_async_remote_copy(
            src_ref=src, dst_ref=dst, send_sem=send, recv_sem=recv,
            device_id=device, device_id_type=MESH,
        )

    mine = block(me)
    copy_walk = pltpu.make_async_copy(walk_hbm, wbuf, c_sem.at[0])
    copy_top = pltpu.make_async_copy(chol_hbm.at[:, pl.ds(0, depth)], top, c_sem.at[1])
    copy_own = pltpu.make_async_copy(chol_hbm.at[:, mine], lrows.at[me], c_sem.at[2])
    copy_walk.start()
    copy_top.start()
    copy_own.start()

    barrier = pltpu.get_barrier_semaphore()

    @pl.loop(1, nchol)
    def _(k):
        pl.semaphore_signal(barrier, inc=1, device_id={"chol": lax.rem(me + k, nchol)}, device_id_type=MESH)

    for shift in (1, -1, 2, -2):
        pl.semaphore_signal(barrier, inc=1, device_id=walk_id(shift), device_id_type=MESH)
    pl.semaphore_wait(barrier, nchol - 1 + 4)

    def l_copy(k, owner, target):
        return remote(chol_hbm.at[core, block(target)], lrows.at[owner, core],
                      l_send.at[k], l_recv.at[k], {"chol": target})

    def f_copy(k, owner, which):
        return remote(lrows.at[owner, which], lrows.at[owner, which],
                      f_send.at[k], f_recv.at[k], {"walk": partner})

    @pl.loop(1, nchol)
    def _(k):
        l_copy(k, me, lax.rem(me + k, nchol)).start()

    copy_walk.wait()
    pall[...] = jnp.zeros_like(pall)
    for i in range(walks):
        pall[i, :, 0:nelec] = wbuf[i, :, 0:nelec]
        pall[i, :, LANES:LANES + nelec] = wbuf[i, :, nelec:2 * nelec]
    for i in range(walks):
        high, low = split(pall[i])
        phi[i] = high
        plo[i] = low

    copy_top.wait()
    top_split = split(top[...].reshape(walks * depth, norb))
    at_row = lax.broadcasted_iota(jnp.int32, (LANES, LANES), 0)
    at_col = lax.broadcasted_iota(jnp.int32, (LANES, LANES), 1)
    unit = jnp.where((at_row == at_col) & (at_row < nelec), 1.0, 0.0).astype(F32)
    unit_row = jnp.concatenate([unit, jnp.zeros_like(unit)], axis=1)
    inside = lax.broadcasted_iota(jnp.int32, (LANES, 2 * LANES), 0) < nelec

    stage = []
    for i in range(walks):
        moment = dot3(top_split, (phi[i], plo[i]))
        err = jnp.where(inside, unit_row - pall[i, 0:LANES, :], 0.0)
        stage.append((moment, err))
    later = []
    for moment, err in stage:
        left = jnp.concatenate([err, moment], axis=0)
        prod = dot3(split(left), split(block_form(err)))
        later.append((prod[:LANES], moment + prod[LANES:]))
    for i, (err2, moment) in enumerate(later):
        left = jnp.concatenate([err2, moment], axis=0)
        prod = dot3(split(left), split(block_form(err2)))
        err4 = prod[:LANES]
        moment = moment + prod[LANES:]
        tr = (unit + err4[:, :LANES]).T[:depth]
        ti = err4[:, LANES:].T[:depth]
        log_part = jnp.zeros((1, 1), F32)
        for g in range(2):
            mr = moment[g * depth:(g + 1) * depth, :LANES]
            mi = moment[g * depth:(g + 1) * depth, LANES:]
            xr = ROOT_DT * jnp.sum(mr * tr - mi * ti, keepdims=True)
            xi = ROOT_DT * jnp.sum(mr * ti + mi * tr, keepdims=True)
            field = fields_s[i, g]
            log_part = log_part + (field * xr - 0.5 * (xr * xr - xi * xi))
            at = 2 * i + g
            msgs[me, at:at + 1, :] = jnp.broadcast_to(ROOT_DT * xi, (1, LANES))
            msgs[me, 4 + at:5 + at, :] = jnp.broadcast_to(ROOT_DT * (field - xr), (1, LANES))
        msgs[me, 8 + i:9 + i, :] = jnp.broadcast_to(log_part, (1, LANES))

    def m_copy(k, owner, target):
        return remote(msgs.at[owner], msgs.at[owner], m_send.at[k], m_recv.at[k], {"chol": target})

    @pl.loop(1, nchol)
    def _(k):
        m_copy(k, me, lax.rem(me + k, nchol)).start()

    @pl.loop(1, nchol)
    def _(k):
        owner = lax.rem(me + nchol - k, nchol)
        l_copy(k, owner, owner).wait_recv()
        f_copy(k, owner, core).start()

    @pl.loop(1, nchol)
    def _(k):
        owner = lax.rem(me + nchol - k, nchol)
        m_copy(k, owner, owner).wait_recv()

    for i in range(walks):
        log_weight = msgs[0, 8 + i:9 + i, :]
        for o in range(1, nchol):
            log_weight = log_weight + msgs[o, 8 + i:9 + i, :]
        ring[0, core, i:i + 1, :] = weights_s[i] * jnp.exp(log_weight)
        ring[0, core, 2 + i:3 + i, :] = jnp.full((1, LANES), counts_s[i].astype(F32))
    half_ring = nchip // 2

    def up_slot(d):
        return d

    def down_slot(d):
        return 0 if d == 0 else half_ring + d

    def ring_start(d):
        if d == 0:
            remote(ring.at[0, core], ring.at[0, core], r_send.at[0], r_recv.at[0], {"walk": partner}).start()
            return
        up, down = up_slot(d), down_slot(d)
        remote(ring.at[up_slot(d - 1)], ring.at[up], r_send.at[up], r_recv.at[up], walk_id(2)).start()
        if d < half_ring:
            remote(ring.at[down_slot(d - 1)], ring.at[down], r_send.at[down], r_recv.at[down], walk_id(-2)).start()

    def ring_wait(d):
        if d == 0:
            remote(ring.at[0, core], ring.at[0, core], r_send.at[0], r_recv.at[0], {"walk": partner}).wait()
            return
        up, down = up_slot(d), down_slot(d)
        remote(ring.at[up_slot(d - 1)], ring.at[up], r_send.at[up], r_recv.at[up], walk_id(2)).wait()
        if d < half_ring:
            remote(ring.at[down_slot(d - 1)], ring.at[down], r_send.at[down], r_recv.at[down], walk_id(-2)).wait()

    ring_start(0)

    @pl.loop(1, nchol)
    def _(k):
        owner = lax.rem(me + nchol - k, nchol)
        f_copy(k, owner, 1 - core).wait_recv()

    copy_own.wait()

    part = rows // 2
    pieces = []
    for h in range(2):
        sums = [jnp.zeros((part, norb), F32) for _ in range(4)]
        for o in range(nchol):
            for g in range(2):
                l = lrows[o, g, h * part:(h + 1) * part, :]
                for i in range(walks):
                    for ri in range(2):
                        at = 4 * ri + 2 * i + g
                        c = jnp.concatenate([msgs[o, at:at + 1, :]] * (norb // LANES), axis=1)
                        sums[2 * i + ri] = sums[2 * i + ri] + c * l
        pieces.append(sums)
    oper = []
    for i in range(walks):
        oper.append(split(jnp.concatenate(
            [pieces[0][2 * i], pieces[1][2 * i], pieces[0][2 * i + 1], pieces[1][2 * i + 1]], axis=0)))

    def g_copy(n, src, dst, k, target):
        return remote(src, dst, g_send.at[n, k], g_recv.at[n, k], {"chol": target})

    for n in range(1, TAYLOR + 1):
        for i in range(walks):
            if n == 1:
                q = (phi[i], plo[i])
            else:
                q = split((q1 if n == 2 else q2)[i])
            y = dot3(oper[i], q)
            low = y[rows:]
            term = (y[:rows] + jnp.concatenate([-low[:, LANES:], low[:, :LANES]], axis=1)) / n
            if n == 1:
                ser[i] = pall[i, mine, :] + term
            else:
                ser[i] = ser[i] + term
            if n < TAYLOR:
                (q1 if n == 1 else q2)[i, mine, :] = term
        if n < TAYLOR:
            q = q1 if n == 1 else q2

            @pl.loop(1, nchol)
            def _(k):
                g_copy(n, q.at[:, mine], q.at[:, mine], k, lax.rem(me + k, nchol)).start()

            for s in range(4):
                d = 4 * (n - 1) + s
                ring_wait(d)
                ring_start(d + 1)

                @pl.loop(1 + 4 * s, min(nchol, 5 + 4 * s))
                def _(k):
                    owner = block(lax.rem(me + nchol - k, nchol))
                    g_copy(n, q.at[:, owner], q.at[:, owner], k, me).wait_recv()

    for side, shift in ((0, 1), (1, -1)):
        remote(ser, near.at[side], n_send.at[side], n_recv.at[side], walk_id(shift)).start()
    ring_wait(half_ring)

    zero = jnp.zeros((1, LANES), F32)
    total, base, base_count = zero, zero, zero
    for d in range(nchip):
        if d == 0:
            earlier = [core == 1, core < 0]
        elif d <= half_ring:
            earlier = [d <= chip] * 2
        else:
            earlier = [chip + (d - half_ring) >= nchip] * 2
        for c in range(2):
            pair = ring[d, c, 0:1, :] + ring[d, c, 1:2, :]
            total = total + pair
            base = base + jnp.where(earlier[c], pair, 0.0)
            base_count = base_count + jnp.where(earlier[c], ring[d, c, 2:3, :] + ring[d, c, 3:4, :], 0.0)
    running = base
    for i in range(walks):
        running = running + ring[0, core, i:i + 1, :]
        comb_s[i] = jnp.max(nwalk * walks * running / total)

    def counts_of(when_even, when_odd, i):
        return jnp.where(core == 0, ring[when_even[0], when_even[1], 2 + i:3 + i, :],
                         ring[when_odd[0], when_odd[1], 2 + i:3 + i, :])

    own_counts = [ring[0, core, 2 + i:3 + i, :] for i in range(walks)]
    left_counts = [counts_of((1, 1), (0, 0), i) for i in range(walks)]
    right_counts = [counts_of((0, 1), (half_ring + 1, 0), i) for i in range(walks)]
    left_start = base_count - left_counts[0] - left_counts[1]
    right_start = base_count + own_counts[0] + own_counts[1]
    weights_of = []
    for start, cs, valid in (
        (base_count, own_counts, w >= 0),
        (left_start, left_counts, w > 0),
        (right_start, right_counts, w < nwalk - 1),
    ):
        for i in range(walks):
            end = start + cs[i]
            picks = []
            for m in range(walks):
                target = jnp.full((1, LANES), (w * walks + m).astype(F32))
                hit = jnp.where(start <= target, 1.0, 0.0) * jnp.where(target < end, 1.0, 0.0)
                picks.append(jnp.where(valid, hit, 0.0))
            weights_of.append(picks)
            start = end
    for side, shift in ((0, 1), (1, -1)):
        remote(ser, near.at[side], n_send.at[side], n_recv.at[side], walk_id(shift)).wait()
    for m in range(walks):
        acc = jnp.zeros((rows, 2 * LANES), F32)
        for j in range(3 * walks):
            i = j % walks
            source = ser[i] if j < walks else near[j // walks - 1, i]
            pick = weights_of[j][m]
            acc = acc + jnp.concatenate([pick, pick], axis=1) * source
        fin[m] = acc

    @pl.loop(1, nchol)
    def _(k):
        g_copy(0, fin, out_ref.at[:, mine], k, lax.rem(me + k, nchol)).start()

    put_own = pltpu.make_async_copy(fin, out_ref.at[:, mine], c_sem.at[3])
    put_own.start()

    @pl.loop(1, nchol)
    def _(k):
        owner = lax.rem(me + nchol - k, nchol)
        l_copy(k, owner, owner).wait_send()
        f_copy(k, owner, core).wait_send()
        m_copy(k, owner, owner).wait_send()
        g_copy(1, q1.at[:, mine], q1.at[:, mine], k, owner).wait_send()
        g_copy(2, q2.at[:, mine], q2.at[:, mine], k, owner).wait_send()

    @pl.loop(1, nchol)
    def _(k):
        owner = lax.rem(me + nchol - k, nchol)
        g_copy(0, fin, out_ref.at[:, block(owner)], k, owner).wait()

    put_own.wait()


def solution(mesh):
    nwalk, nchol = mesh.shape["walk"], mesh.shape["chol"]

    def on_device(walkers, cholesky, fields, weights, counts):
        walks, norb, width = walkers.shape
        nelec = width // 2
        ng = cholesky.shape[0]
        rows = norb // nchol
        depth = -(-nelec // 8) * 8
        vmem = pltpu.VMEM
        dma = pltpu.SemaphoreType.DMA
        smem = pl.BlockSpec(memory_space=pltpu.SMEM)
        hbm = pl.BlockSpec(memory_space=pl.ANY)
        padded, comb = pl.pallas_call(
            functools.partial(kernel, nwalk, nchol, nelec),
            out_shape=(
                jax.ShapeDtypeStruct((walks, norb, 2 * LANES), F32),
                jax.ShapeDtypeStruct((walks,), F32),
            ),
            in_specs=[hbm, hbm, smem, smem, smem],
            out_specs=(hbm, smem),
            scratch_shapes=[
                vmem((walks, norb, width), F32),
                vmem((ng, depth, norb), F32),
                vmem((nchol, ng, rows, norb), F32),
                vmem((walks, norb, 2 * LANES), F32),
                vmem((walks, norb, 2 * LANES), BF16),
                vmem((walks, norb, 2 * LANES), BF16),
                vmem((nchol, 16, LANES), F32),
                vmem((walks, norb, 2 * LANES), F32),
                vmem((walks, norb, 2 * LANES), F32),
                vmem((walks, rows, 2 * LANES), F32),
                vmem((walks, rows, 2 * LANES), F32),
                vmem((2, walks, rows, 2 * LANES), F32),
                vmem((nwalk // 2, 2, 8, LANES), F32),
                dma((4,)),
                dma((nchol,)), dma((nchol,)), dma((nchol,)), dma((nchol,)), dma((nchol,)), dma((nchol,)),
                dma((3, nchol)), dma((3, nchol)),
                dma((nwalk // 2,)), dma((nwalk // 2,)),
                dma((2,)), dma((2,)),
            ],
            compiler_params=pltpu.CompilerParams(collective_id=0, has_side_effects=True),
        )(walkers, cholesky, fields, weights, counts)
        routed = jnp.concatenate([padded[..., :nelec], padded[..., LANES:LANES + nelec]], axis=-1)
        return routed, comb

    in_specs = (P("walk", None, None), P("chol", None, None), P("walk", "chol"), P("walk"), P("walk"))
    return jax.shard_map(
        on_device, mesh=mesh, in_specs=in_specs, out_specs=(P("walk", None, None), P("walk")), check_vma=False
    )
```

time: 536 us -> 94.5 us (0.18)
  the two profiles are of different devices: /device:TPU:480 before, /device:TPU:8 now
where the time goes in v1:
time: 94.5 us; the launch traced here: 94.2 us
  Pallas kernels  87.8 us (93%)
  local copies, waits for them, and re-layouts  5.46 us (6%)
    pallas_call x1, Pallas kernels, on_device(): pl.pallas_call(functools.partial(kernel, nwalk, nchol, nelec), out_shape=...  87.8 us
    unnamed x5, local copies, waits for them, and re-layouts  4.19 us

profile of v1, /device:TPU:8, one launch (start us, length us, event | category | flops | bytes accessed | tf_op | source)
XLA Modules:
  0.0 94.2 jit_solution(4895963172127868840)
XLA Ops:
  0.6 2.5 %copy.7.walk_hbm = f32[2,512,200]{2,1,0:T(8,128)} copy(f32[2,512,200]{1,2,0:T(8,128)} %param.5) | data formatting | bytes 1638400 | tf_op args[0]
  3.1 87.8 %shard_map.68 = (f32[2,512,256]{2,1,0:T(8,128)}, f32[2]{0:T(128)}) custom-call(f32[2,512,200]{2,1,0:T(8,128)} %copy.7.walk_hbm, f32[2,512,512]{2,1,0:T(8,128)} %chol_hbm.1, f32[2,2]{1,0:T(2,128)} %fields_s.1, f32[2]{0:T(128)} %weights_s.1, s32[2]{0:T(128)} %counts_s.1), custom_call_target="tpu_custom_call" | custom-call | tf_op jit(solution)/shard_map/pallas_call | solution.py:351
  90.9 1.3 %fusion = (f32[2,512,100]{2,1,0:T(8,128)S(1)}, f32[2,512,100]{2,1,0:T(8,128)S(1)}) fusion(f32[2,512,256]{2,1,0:T(8,128)} %get-tuple-element.4), kind=kLoop, calls=%fused_computation.1 | loop fusion | bytes 1638400 | tf_op jit(solution)/shard_map/slice | solution.py:381
  92.2 0.0 copy-start
  92.2 0.3 pad_maximum_fusion
  92.5 1.2 %copy.8 = f32[2,512,200]{1,2,0:T(8,128)} copy(f32[2,512,200]{2,1,0:T(8,128)S(1)} %pad_maximum_fusion) | data formatting | bytes 1638400
  93.7 0.0 copy-done
  93.7 0.5 copy.10
Async XLA Ops:
  92.2 1.6 %copy-start = (f32[2]{0:T(128)S(1)}, f32[2]{0:T(128)}, u32[]{:S(2)}) copy-start(f32[2]{0:T(128)} %get-tuple-element.13) | copy-start | bytes 28

commit v2 on v1

v2 whole, which is shorter than its diff:
```python
import functools

import jax
import jax.numpy as jnp
from jax import lax
from jax.experimental import pallas as pl
from jax.experimental.pallas import tpu as pltpu
from jax.sharding import PartitionSpec as P

F32 = jnp.float32
BF16 = jnp.bfloat16
MESH = pl.DeviceIdType.MESH
TAYLOR = 3
LANES = 128
ROOT_DT = 0.1


def split(a):
    high = a.astype(BF16)
    return high, (a - high.astype(F32)).astype(BF16)


def dot(a, b):
    return jnp.dot(a, b, preferred_element_type=F32)


def dot3(a, b):
    return dot(a[0], b[0]) + (dot(a[1], b[0]) + dot(a[0], b[1]))


def block_form(c):
    re, im = c[:, :LANES], c[:, LANES:]
    return jnp.concatenate([c, jnp.concatenate([-im, re], axis=1)], axis=0)


def kernel(
    nwalk, nchol, nelec,
    walk_hbm, chol_hbm, fields_s, weights_s, counts_s,
    out_ref, comb_s,
    wbuf, padt, top, lrows, pall, phi, plo, msgs, acomp, abuf, q0, q1, q2, cand, qf, ring,
    c_sem, l_send, l_recv, z_send, z_recv, f_send, f_recv, m_send, m_recv,
    a_send, a_recv, g_send, g_recv, o_send, o_recv, r_send, r_recv, n_send, n_recv,
):
    w = lax.axis_index("walk")
    me = lax.axis_index("chol")
    core = lax.rem(w, 2)
    chip = lax.div(w, 2)
    nchip = nwalk // 2
    partner = w + 1 - 2 * core
    walks, norb = wbuf.shape[0], wbuf.shape[2]
    rows = norb // nchol
    depth = top.shape[1]
    half = rows // 2
    side = 4
    gx, gy = lax.rem(me, side), lax.div(me, side)
    parity = lax.rem(chip, 2)
    band = rows * side
    mine_walker, mine_half = lax.div(gy, 2), lax.rem(gy, 2)
    first = -(-nelec // 16) * 8
    quarter = LANES // 2

    def walk_id(shift):
        return {"walk": lax.rem(w + nwalk + shift, nwalk)}

    def chip_id(shift, which):
        return {"walk": 2 * lax.rem(chip + nchip + shift, nchip) + which}

    def block(owner):
        at = lax.rem(owner, side) * side + lax.div(owner, side)
        return pl.ds(pl.multiple_of(at * rows, rows), rows)

    def at_band(bx):
        return pl.ds(pl.multiple_of(bx * band, band), band)

    def chip_at(dx, dy):
        return lax.rem(gy + side + dy, side) * side + lax.rem(gx + side + dx, side)

    def remote(src, dst, send, recv, device):
        return pltpu.make_async_remote_copy(
            src_ref=src, dst_ref=dst, send_sem=send, recv_sem=recv,
            device_id=device, device_id_type=MESH,
        )

    mine = block(me)
    copy_walk = pltpu.make_async_copy(walk_hbm, wbuf, c_sem.at[0])
    copy_top = pltpu.make_async_copy(chol_hbm.at[:, pl.ds(0, depth)], top, c_sem.at[1])
    copy_own = pltpu.make_async_copy(chol_hbm.at[:, mine], lrows.at[me], c_sem.at[2])
    copy_walk.start()
    copy_top.start()
    copy_own.start()

    barrier = pltpu.get_barrier_semaphore()

    @pl.loop(1, nchol)
    def _(k):
        pl.semaphore_signal(barrier, inc=1, device_id={"chol": lax.rem(me + k, nchol)}, device_id_type=MESH)

    greet = [{"walk": partner}]
    for shift in (1, -1):
        greet += [chip_id(shift, core), chip_id(shift, 1 - core)]
    for shift in (3, -3, 4, -4):
        greet.append(chip_id(shift, core))
    for shift in (1, -1):
        greet.append({**walk_id(shift), "chol": chip_at(0, 2)})
    for device in greet:
        pl.semaphore_signal(barrier, inc=1, device_id=device, device_id_type=MESH)
    pl.semaphore_wait(barrier, nchol - 1 + len(greet))

    def piece(owner, which, part):
        return lrows.at[owner, which, pl.ds(pl.multiple_of(part * half, 8), half)]

    def l_copy(k, owner, target):
        return remote(chol_hbm.at[core, pl.ds(pl.multiple_of(
            (lax.rem(target, side) * side + lax.div(target, side)) * rows + parity * half, 8), half)],
                      piece(owner, core, parity), l_send.at[k], l_recv.at[k], {"chol": target})

    def z_copy(k, owner, part):
        return remote(piece(owner, core, part), piece(owner, core, part), z_send.at[k], z_recv.at[k],
                      chip_id(2 * lax.rem(owner, 2) - 1, core))

    def f_copy(k, owner, which, part, slot):
        return remote(piece(owner, which, part), piece(owner, which, part),
                      f_send.at[slot, k], f_recv.at[slot, k], {"walk": partner})

    @pl.loop(1, nchol)
    def _(k):
        l_copy(k, me, lax.rem(me + k, nchol)).start()

    copy_walk.wait()
    for i in range(walks):
        padt[i, 96:LANES, :] = jnp.zeros((LANES - 96, norb), F32)
        padt[i, LANES + 96:2 * LANES, :] = jnp.zeros((LANES - 96, norb), F32)
        padt[i, 0:nelec, :] = wbuf[i, 0:nelec, :]
        padt[i, LANES:LANES + nelec, :] = wbuf[i, nelec:2 * nelec, :]
    for i in range(walks):
        pall[i] = padt[i].T
        high, low = split(pall[i])
        phi[i] = high
        plo[i] = low

    copy_top.wait()
    top_split = split(top[...].reshape(walks * depth, norb))
    at_row = lax.broadcasted_iota(jnp.int32, (LANES, LANES), 0)
    at_col = lax.broadcasted_iota(jnp.int32, (LANES, LANES), 1)
    unit = jnp.where((at_row == at_col) & (at_row < nelec), 1.0, 0.0).astype(F32)
    unit_row = jnp.concatenate([unit, jnp.zeros_like(unit)], axis=1)
    inside = lax.broadcasted_iota(jnp.int32, (LANES, 2 * LANES), 0) < nelec

    stage = []
    for i in range(walks):
        moment = dot3(top_split, (phi[i], plo[i]))
        err = jnp.where(inside, unit_row - pall[i, 0:LANES, :], 0.0)
        stage.append((moment, err))
    later = []
    for moment, err in stage:
        left = jnp.concatenate([err, moment], axis=0)
        prod = dot3(split(left), split(block_form(err)))
        later.append((prod[:LANES], moment + prod[LANES:]))
    for i, (err2, moment) in enumerate(later):
        left = jnp.concatenate([err2, moment], axis=0)
        prod = dot3(split(left), split(block_form(err2)))
        err4 = prod[:LANES]
        moment = moment + prod[LANES:]
        tr = (unit + err4[:, :LANES]).T[:depth]
        ti = err4[:, LANES:].T[:depth]
        log_part = jnp.zeros((1, 1), F32)
        for g in range(2):
            mr = moment[g * depth:(g + 1) * depth, :LANES]
            mi = moment[g * depth:(g + 1) * depth, LANES:]
            xr = ROOT_DT * jnp.sum(mr * tr - mi * ti, keepdims=True)
            xi = ROOT_DT * jnp.sum(mr * ti + mi * tr, keepdims=True)
            field = fields_s[i, g]
            log_part = log_part + (field * xr - 0.5 * (xr * xr - xi * xi))
            at = 2 * i + g
            msgs[me, at:at + 1, :] = jnp.broadcast_to(ROOT_DT * xi, (1, LANES))
            msgs[me, 4 + at:5 + at, :] = jnp.broadcast_to(ROOT_DT * (field - xr), (1, LANES))
        msgs[me, 8 + i:9 + i, :] = jnp.broadcast_to(log_part, (1, LANES))

    def m_copy(k, owner, target):
        return remote(msgs.at[owner], msgs.at[owner], m_send.at[k], m_recv.at[k], {"chol": target})

    @pl.loop(1, nchol)
    def _(k):
        m_copy(k, me, lax.rem(me + k, nchol)).start()

    @pl.loop(1, nchol)
    def _(k):
        owner = lax.rem(me + nchol - k, nchol)
        l_copy(k, owner, owner).wait_recv()
        z_copy(k, owner, parity).start()
        f_copy(k, owner, core, parity, 0).start()

    @pl.loop(1, nchol)
    def _(k):
        owner = lax.rem(me + nchol - k, nchol)
        z_copy(k, owner, 1 - parity).wait_recv()
        f_copy(k, owner, core, 1 - parity, 1).start()

    @pl.loop(1, nchol)
    def _(k):
        owner = lax.rem(me + nchol - k, nchol)
        m_copy(k, owner, owner).wait_recv()

    here = nchip // 2
    for i in range(walks):
        log_weight = msgs[0, 8 + i:9 + i, :]
        for o in range(1, nchol):
            log_weight = log_weight + msgs[o, 8 + i:9 + i, :]
        ring[here, core, i:i + 1, :] = weights_s[i] * jnp.exp(log_weight)
        ring[here, core, 2 + i:3 + i, :] = jnp.full((1, LANES), counts_s[i].astype(F32))

    def spread(stage):
        if stage == 0:
            own = ring.at[here, core]
            return [remote(own, own, r_send.at[0], r_recv.at[0], {"walk": partner})] + [
                remote(own, ring.at[here - d, core], r_send.at[j], r_recv.at[j], chip_id(d, c))
                for j, d, c in ((1, 1, core), (2, 1, 1 - core), (3, -1, core), (4, -1, 1 - core))]
        if stage == 1:
            return [remote(ring.at[here - 1:here + 2], ring.at[here - d - 1:here - d + 2],
                           r_send.at[j], r_recv.at[j], chip_id(d, core)) for j, d in ((5, 3), (6, -3))]
        return [remote(ring.at[here - 4:here], ring.at[here - 8:here - 4], r_send.at[7], r_recv.at[7], chip_id(4, core)),
                remote(ring.at[here + 1:here + 4], ring.at[here + 5:here + 8], r_send.at[8], r_recv.at[8], chip_id(-4, core))]

    def spread_start(stage):
        for copy in spread(stage):
            copy.start()

    def spread_wait(stage):
        for copy in spread(stage):
            copy.wait()

    spread_start(0)

    @pl.loop(1, nchol)
    def _(k):
        owner = lax.rem(me + nchol - k, nchol)
        f_copy(k, owner, 1 - core, parity, 0).wait_recv()
        f_copy(k, owner, 1 - core, 1 - parity, 1).wait_recv()

    copy_own.wait()

    part = rows // 2
    pieces = []
    for h in range(2):
        sums = [jnp.zeros((part, norb), F32) for _ in range(4)]
        for o in range(nchol):
            for g in range(2):
                l = lrows[o, g, h * part:(h + 1) * part, :]
                for i in range(walks):
                    for ri in range(2):
                        at = 4 * ri + 2 * i + g
                        c = jnp.concatenate([msgs[o, at:at + 1, :]] * (norb // LANES), axis=1)
                        sums[2 * i + ri] = sums[2 * i + ri] + c * l
        pieces.append(sums)
    for i in range(walks):
        for ri in range(2):
            for h in range(2):
                acomp[i, ri, h * part:(h + 1) * part, :] = pieces[h][2 * i + ri]

    def band_rows(by):
        return pl.ds(pl.multiple_of(by * rows, rows), rows)

    def a_copy(d):
        to = lax.rem(gy + d, side)
        return remote(acomp.at[lax.div(to, 2)], abuf.at[:, band_rows(gy)], a_send.at[d], a_recv.at[d],
                      {"chol": chip_at(0, d)})

    for d in (2, 1, 3):
        a_copy(d).start()
    abuf[:, band_rows(gy), :] = acomp[mine_walker]
    cols = pl.multiple_of(mine_half * first, 8)
    q0[...] = jnp.concatenate(
        [padt[mine_walker, pl.ds(cols, quarter), :], padt[mine_walker, pl.ds(LANES + cols, quarter), :]], axis=0).T
    spread_wait(0)
    spread_start(1)
    q_split = split(q0[...])
    for d in (1, 3, 2):
        a_copy(d).wait_recv()
    oper = split(abuf[...].reshape(2 * band, norb))
    minus = jnp.where(lax.broadcasted_iota(jnp.int32, (band, LANES), 1) < quarter, -1.0, 1.0).astype(F32)

    def g_copy(n, q, d):
        ref = q.at[at_band(gx)]
        return remote(ref, ref, g_send.at[n, d], g_recv.at[n, d], {"chol": chip_at(d, 0)})

    series = q0[at_band(gx), :]
    for n in range(1, TAYLOR + 1):
        prod = dot3(oper, q_split)
        term = (prod[:band] + minus * pltpu.roll(prod[band:], quarter, 1)) / n
        series = series + term
        if n < TAYLOR:
            q = q1 if n == 1 else q2
            q[at_band(gx), :] = term
            for d in (2, 1, 3):
                g_copy(n - 1, q, d).start()
            if n == 1:
                spread_wait(1)
                spread_start(2)
            for d in (1, 3, 2):
                g_copy(n - 1, q, d).wait_recv()
            q_split = split(q[...])
    cand[mine_walker] = series

    def near_copy(j):
        shift = (0, 1, 1, -1, -1)[j]
        device = {"chol": chip_at(0, 0 if j in (1, 3) else 2)}
        if shift:
            device.update(walk_id(shift))
        return remote(cand.at[mine_walker], cand.at[2 * (0, 1, 1, 2, 2)[j] + mine_walker],
                      n_send.at[j], n_recv.at[j], device)

    for j in (2, 4, 0, 1, 3):
        near_copy(j).start()
    spread_wait(2)

    zero = jnp.zeros((1, LANES), F32)
    total, base, base_count = zero, zero, zero
    for d in range(-here, here):
        if d == 0:
            earlier = [core == 1, core < 0]
        elif d < 0:
            earlier = [chip + d >= 0] * 2
        else:
            earlier = [chip + d >= nchip] * 2
        for c in range(2):
            pair = ring[here + d, c, 0:1, :] + ring[here + d, c, 1:2, :]
            total = total + pair
            base = base + jnp.where(earlier[c], pair, 0.0)
            base_count = base_count + jnp.where(
                earlier[c], ring[here + d, c, 2:3, :] + ring[here + d, c, 3:4, :], 0.0)
    running = base
    for i in range(walks):
        running = running + ring[here, core, i:i + 1, :]
        comb_s[i] = jnp.max(nwalk * walks * running / total)

    def counts_of(when_even, when_odd, i):
        return jnp.where(core == 0, ring[when_even[0], when_even[1], 2 + i:3 + i, :],
                         ring[when_odd[0], when_odd[1], 2 + i:3 + i, :])

    own_counts = [ring[here, core, 2 + i:3 + i, :] for i in range(walks)]
    left_counts = [counts_of((here - 1, 1), (here, 0), i) for i in range(walks)]
    right_counts = [counts_of((here, 1), (here + 1, 0), i) for i in range(walks)]
    left_start = base_count - left_counts[0] - left_counts[1]
    right_start = base_count + own_counts[0] + own_counts[1]
    weights_of = []
    for start, cs, valid in (
        (base_count, own_counts, w >= 0),
        (left_start, left_counts, w > 0),
        (right_start, right_counts, w < nwalk - 1),
    ):
        for i in range(walks):
            end = start + cs[i]
            target = jnp.full((1, LANES), (w * walks + mine_walker).astype(F32))
            hit = jnp.where(start <= target, 1.0, 0.0) * jnp.where(target < end, 1.0, 0.0)
            weights_of.append(jnp.where(valid, hit, 0.0))
            start = end
    def o_copy(c, sem, origin, to):
        (da, db), (ta, tb) = origin, to
        dx, dy = (da, db) if c == 0 else (db, da)
        tx, ty = (ta, tb) if c == 0 else (tb, ta)
        ref = qf.at[lax.rem(gy + side + dy, side),
                    pl.ds(pl.multiple_of(lax.rem(gx + side + dx, side) * band + c * (band // 2), band // 2), band // 2)]
        return remote(ref, ref, o_send.at[c, sem], o_recv.at[c, sem], {"chol": chip_at(tx, ty)})

    def o_send_first(c, d):
        return o_copy(c, d, (0, 0), (d, 0))

    def o_send_second(c, d, e):
        return o_copy(c, 4 * d + e, (-d, 0), (0, e)) if d else o_copy(c, 16 + e, (0, 0), (0, e))

    def o_recv_first(c, d):
        return o_copy(c, d, (-d, 0), (d, 0))

    def o_recv_second(c, d, e):
        return o_copy(c, 4 * d + e, (-d, -e), (0, e)) if d else o_copy(c, 16 + e, (0, -e), (0, e))

    for j in range(5):
        near_copy(j).wait_send()
    for j in range(5):
        shift = (0, 1, 1, -1, -1)[j]
        slot = 2 * (0, 1, 1, 2, 2)[j] + (mine_walker if j in (1, 3) else 1 - mine_walker)
        remote(cand.at[slot], cand.at[slot], n_send.at[j], n_recv.at[j], walk_id(1)).wait_recv()
    acc = jnp.zeros((band, LANES), F32)
    for j in range(3 * walks):
        acc = acc + weights_of[j] * cand[j]
    qf[gy, at_band(gx), :] = acc
    for d in (2, 1, 3):
        for c in range(2):
            o_send_first(c, d).start()
    for d in (2, 1, 3):
        for c in range(2):
            o_send_second(c, 0, d).start()
    for d in (1, 3, 2):
        for c in range(2):
            o_recv_first(c, d).wait_recv()
            for e in (2, 1, 3):
                o_send_second(c, d, e).start()
    for c in range(2):
        for d in (0, 1, 3, 2):
            for e in (1, 3, 2):
                o_recv_second(c, d, e).wait_recv()
    rest = nelec - first
    for i in range(walks):
        for h in range(2):
            turned = qf[2 * i + h].T
            size = rest if h else first
            wbuf[i, h * first:h * first + size, :] = turned[:size]
            wbuf[i, nelec + h * first:nelec + h * first + size, :] = turned[quarter:quarter + size]
        pltpu.make_async_copy(wbuf.at[i], out_ref.at[i], c_sem.at[3 + i]).start()

    @pl.loop(1, nchol)
    def _(k):
        owner = lax.rem(me + nchol - k, nchol)
        l_copy(k, owner, owner).wait_send()
        z_copy(k, owner, parity).wait_send()
        f_copy(k, owner, core, parity, 0).wait_send()
        f_copy(k, owner, core, 1 - parity, 1).wait_send()
        m_copy(k, owner, owner).wait_send()

    for d in range(1, side):
        a_copy(d).wait_send()
        g_copy(0, q1, d).wait_send()
        g_copy(1, q2, d).wait_send()
        for c in range(2):
            o_send_first(c, d).wait_send()
            for e in range(side):
                o_send_second(c, e, d).wait_send()
    for i in range(walks):
        pltpu.make_async_copy(wbuf.at[i], out_ref.at[i], c_sem.at[3 + i]).wait()


def solution(mesh):
    nwalk, nchol = mesh.shape["walk"], mesh.shape["chol"]

    def on_device(walkers, cholesky, fields, weights, counts):
        walks, norb, width = walkers.shape
        nelec = width // 2
        ng = cholesky.shape[0]
        rows = norb // nchol
        depth = -(-nelec // 8) * 8
        vmem = pltpu.VMEM
        dma = pltpu.SemaphoreType.DMA
        smem = pl.BlockSpec(memory_space=pltpu.SMEM)
        hbm = pl.BlockSpec(memory_space=pl.ANY)
        routed, comb = pl.pallas_call(
            functools.partial(kernel, nwalk, nchol, nelec),
            out_shape=(
                jax.ShapeDtypeStruct((walks, width, norb), F32),
                jax.ShapeDtypeStruct((walks,), F32),
            ),
            in_specs=[hbm, hbm, smem, smem, smem],
            out_specs=(hbm, smem),
            scratch_shapes=[
                vmem((walks, width, norb), F32),
                vmem((walks, 2 * LANES, norb), F32),
                vmem((ng, depth, norb), F32),
                vmem((nchol, ng, rows, norb), F32),
                vmem((walks, norb, 2 * LANES), F32),
                vmem((walks, norb, 2 * LANES), BF16),
                vmem((walks, norb, 2 * LANES), BF16),
                vmem((nchol, 16, LANES), F32),
                vmem((walks, 2, rows, norb), F32),
                vmem((2, 4 * rows, norb), F32),
                vmem((norb, LANES), F32),
                vmem((norb, LANES), F32),
                vmem((norb, LANES), F32),
                vmem((3 * walks, 4 * rows, LANES), F32),
                vmem((4, norb, LANES), F32),
                vmem((nwalk // 2, 2, 8, LANES), F32),
                dma((5,)),
                dma((nchol,)), dma((nchol,)), dma((nchol,)), dma((nchol,)),
                dma((2, nchol)), dma((2, nchol)), dma((nchol,)), dma((nchol,)),
                dma((4,)), dma((4,)), dma((2, 4)), dma((2, 4)), dma((2, 20)), dma((2, 20)),
                dma((9,)), dma((9,)),
                dma((5,)), dma((5,)),
            ],
            compiler_params=pltpu.CompilerParams(collective_id=0, has_side_effects=True),
        )(jnp.swapaxes(walkers, 1, 2), cholesky, fields, weights, counts)
        return jnp.swapaxes(routed, 1, 2), comb

    in_specs = (P("walk", None, None), P("chol", None, None), P("walk", "chol"), P("walk"), P("walk"))
    return jax.shard_map(
        on_device, mesh=mesh, in_specs=in_specs, out_specs=(P("walk", None, None), P("walk")), check_vma=False
    )
```

time: 94.5 us -> 73.8 us (0.78)
  the two profiles are of different devices: /device:TPU:8 before, /device:TPU:1 now
where the time goes in v2:
time: 73.8 us; the launch traced here: 73.6 us
  Pallas kernels  69.7 us (94%)
  local copies, waits for them, and re-layouts  3.26 us (4%)
    pallas_call x1, Pallas kernels, on_device(): pl.pallas_call(functools.partial(kernel, nwalk, nchol, nelec), out_shape=...  69.7 us
    unnamed x2, local copies, waits for them, and re-layouts  3.26 us

profile of v2, /device:TPU:1, one launch (start us, length us, event | category | flops | bytes accessed | tf_op | source)
XLA Modules:
  0.0 73.6 jit_solution(10878587303029866783)
XLA Ops:
  0.6 69.7 %shard_map.68 = (f32[2,200,512]{2,1,0:T(8,128)}, f32[2]{0:T(128)}) custom-call(f32[2,200,512]{2,1,0:T(8,128)} %bitcast.2, f32[2,512,512]{2,1,0:T(8,128)} %chol_hbm.1, f32[2,2]{1,0:T(2,128)} %fields_s.1, f32[2]{0:T(128)} %weights_s.1, s32[2]{0:T(128)} %counts_s.1), custom_call_target="tpu_custom_call" | custom-call | tf_op jit(solution)/shard_map/pallas_call | solution.py:445
  70.3 2.1 %copy.9 = f32[2,512,200]{1,2,0:T(8,128)} copy(f32[2,512,200]{1,2,0:T(8,128)} %bitcast.3) | data formatting | bytes 1638400
  72.4 1.2 %copy.10 = f32[2]{0:T(128)} copy(f32[2]{0:T(128)} %get-tuple-element.9) | data formatting | bytes 16

commit v3 on v2

v3 whole, which is shorter than its diff:
```python
import functools

import jax
import jax.numpy as jnp
from jax import lax
from jax.experimental import pallas as pl
from jax.experimental.pallas import tpu as pltpu
from jax.sharding import PartitionSpec as P

F32 = jnp.float32
BF16 = jnp.bfloat16
MESH = pl.DeviceIdType.MESH
TAYLOR = 3
LANES = 128
ROOT_DT = 0.1


def split(a):
    high = a.astype(BF16)
    return high, (a - high.astype(F32)).astype(BF16)


def dot(a, b):
    return jnp.dot(a, b, preferred_element_type=F32)


def dot3(a, b):
    return dot(a[0], b[0]) + (dot(a[1], b[0]) + dot(a[0], b[1]))


def block_form(c):
    re, im = c[:, :LANES], c[:, LANES:]
    return jnp.concatenate([c, jnp.concatenate([-im, re], axis=1)], axis=0)


def kernel(
    nwalk, nchol, nelec,
    walk_hbm, chol_hbm, fields_s, weights_s, counts_s,
    out_ref, comb_s,
    wbuf, padt, top, lrows, pall, phi, plo, msgs, acomp, abuf, q0, q1, q2, cnew, pcand, qf, ring, tally,
    c_sem, l_send, l_recv, z_send, z_recv, f_send, f_recv, m_send, m_recv,
    a_send, a_recv, s_send, s_recv, g_send, g_recv, o_send, o_recv, r_send, r_recv, t_send, t_recv, n_send, n_recv,
):
    w = lax.axis_index("walk")
    me = lax.axis_index("chol")
    core = lax.rem(w, 2)
    chip = lax.div(w, 2)
    nchip = nwalk // 2
    partner = w + 1 - 2 * core
    walks, norb = wbuf.shape[0], wbuf.shape[2]
    rows = norb // nchol
    depth = top.shape[1]
    half = rows // 2
    side = 4
    gx, gy = lax.rem(me, side), lax.div(me, side)
    parity = lax.rem(chip, 2)
    band = rows * side
    mine_walker, mine_half = lax.div(gy, 2), lax.rem(gy, 2)
    first = -(-nelec // 16) * 8
    quarter = LANES // 2

    def walk_id(shift):
        return {"walk": lax.rem(w + nwalk + shift, nwalk)}

    def chip_id(shift, which):
        return {"walk": 2 * lax.rem(chip + nchip + shift, nchip) + which}

    def block(owner):
        at = lax.rem(owner, side) * side + lax.div(owner, side)
        return pl.ds(pl.multiple_of(at * rows, rows), rows)

    def at_band(bx):
        return pl.ds(pl.multiple_of(bx * band, band), band)

    def chip_at(dx, dy):
        return lax.rem(gy + side + dy, side) * side + lax.rem(gx + side + dx, side)

    def remote(src, dst, send, recv, device):
        return pltpu.make_async_remote_copy(
            src_ref=src, dst_ref=dst, send_sem=send, recv_sem=recv,
            device_id=device, device_id_type=MESH,
        )

    mine = block(me)
    copy_walk = pltpu.make_async_copy(walk_hbm, wbuf, c_sem.at[0])
    copy_top = pltpu.make_async_copy(chol_hbm.at[:, pl.ds(0, depth)], top, c_sem.at[1])
    copy_own = pltpu.make_async_copy(chol_hbm.at[:, mine], lrows.at[me], c_sem.at[2])
    copy_walk.start()
    copy_top.start()
    copy_own.start()

    barrier = pltpu.get_barrier_semaphore()

    @pl.loop(1, nchol)
    def _(k):
        pl.semaphore_signal(barrier, inc=1, device_id={"chol": lax.rem(me + k, nchol)}, device_id_type=MESH)

    greet = [{"walk": partner}]
    for shift in (1, -1):
        greet += [chip_id(shift, core), chip_id(shift, 1 - core)]
    for shift in (3, -3, 4, -4):
        greet.append(chip_id(shift, core))
    for device in greet:
        pl.semaphore_signal(barrier, inc=1, device_id=device, device_id_type=MESH)
    pl.semaphore_wait(barrier, nchol - 1 + len(greet))

    def piece(owner, which, part):
        return lrows.at[owner, which, pl.ds(pl.multiple_of(part * half, 8), half)]

    def l_copy(k, owner, target):
        return remote(chol_hbm.at[core, pl.ds(pl.multiple_of(
            (lax.rem(target, side) * side + lax.div(target, side)) * rows + parity * half, 8), half)],
                      piece(owner, core, parity), l_send.at[k], l_recv.at[k], {"chol": target})

    def z_copy(k, owner, part):
        return remote(piece(owner, core, part), piece(owner, core, part), z_send.at[k], z_recv.at[k],
                      chip_id(2 * lax.rem(owner, 2) - 1, core))

    def f_copy(k, owner, which, part, slot):
        return remote(piece(owner, which, part), piece(owner, which, part),
                      f_send.at[slot, k], f_recv.at[slot, k], {"walk": partner})

    @pl.loop(1, nchol)
    def _(k):
        l_copy(k, me, lax.rem(me + k, nchol)).start()

    here = nchip // 2

    def spread(buf, send, recv, stage):
        if stage == 0:
            own = buf.at[here, core]
            return [remote(own, own, send.at[0], recv.at[0], {"walk": partner})] + [
                remote(own, buf.at[here - d, core], send.at[j], recv.at[j], chip_id(d, c))
                for j, d, c in ((1, 1, core), (2, 1, 1 - core), (3, -1, core), (4, -1, 1 - core))]
        if stage == 1:
            return [remote(buf.at[here - 1:here + 2], buf.at[here - d - 1:here - d + 2],
                           send.at[j], recv.at[j], chip_id(d, core)) for j, d in ((5, 3), (6, -3))]
        return [remote(buf.at[here - 4:here], buf.at[here - 8:here - 4], send.at[7], recv.at[7], chip_id(4, core)),
                remote(buf.at[here + 1:here + 4], buf.at[here + 5:here + 8], send.at[8], recv.at[8], chip_id(-4, core))]

    weights_run, counts_run = (ring, r_send, r_recv), (tally, t_send, t_recv)

    def spread_start(run, stage):
        for copy in spread(*run, stage):
            copy.start()

    def spread_wait(run, stage):
        for copy in spread(*run, stage):
            copy.wait()

    for i in range(walks):
        tally[here, core, i:i + 1, :] = jnp.full((1, LANES), counts_s[i].astype(F32))
    spread_start(counts_run, 0)

    copy_walk.wait()
    for i in range(walks):
        padt[i, :, 96:LANES, :] = jnp.zeros((2, LANES - 96, norb), F32)
        padt[i, 0, 0:nelec, :] = wbuf[i, 0:nelec, :]
        padt[i, 1, 0:nelec, :] = wbuf[i, nelec:2 * nelec, :]
    for i in range(walks):
        pall[i] = padt[i].reshape(2 * LANES, norb).T
        high, low = split(pall[i])
        phi[i] = high
        plo[i] = low

    copy_top.wait()
    top_split = split(top[...].reshape(walks * depth, norb))
    at_row = lax.broadcasted_iota(jnp.int32, (LANES, LANES), 0)
    at_col = lax.broadcasted_iota(jnp.int32, (LANES, LANES), 1)
    unit = jnp.where((at_row == at_col) & (at_row < nelec), 1.0, 0.0).astype(F32)
    unit_row = jnp.concatenate([unit, jnp.zeros_like(unit)], axis=1)
    inside = lax.broadcasted_iota(jnp.int32, (LANES, 2 * LANES), 0) < nelec

    stage = []
    for i in range(walks):
        moment = dot3(top_split, (phi[i], plo[i]))
        err = jnp.where(inside, unit_row - pall[i, 0:LANES, :], 0.0)
        stage.append((moment, err))
    later = []
    for moment, err in stage:
        left = jnp.concatenate([err, moment], axis=0)
        prod = dot3(split(left), split(block_form(err)))
        later.append((prod[:LANES], moment + prod[LANES:]))
    for i, (err2, moment) in enumerate(later):
        left = jnp.concatenate([err2, moment], axis=0)
        prod = dot3(split(left), split(block_form(err2)))
        err4 = prod[:LANES]
        moment = moment + prod[LANES:]
        tr = (unit + err4[:, :LANES]).T[:depth]
        ti = err4[:, LANES:].T[:depth]
        log_part = jnp.zeros((1, 1), F32)
        for g in range(2):
            mr = moment[g * depth:(g + 1) * depth, :LANES]
            mi = moment[g * depth:(g + 1) * depth, LANES:]
            xr = ROOT_DT * jnp.sum(mr * tr - mi * ti, keepdims=True)
            xi = ROOT_DT * jnp.sum(mr * ti + mi * tr, keepdims=True)
            field = fields_s[i, g]
            log_part = log_part + (field * xr - 0.5 * (xr * xr - xi * xi))
            at = 2 * i + g
            msgs[0, me, at:at + 1, :] = jnp.broadcast_to(ROOT_DT * xi, (1, LANES))
            msgs[0, me, 4 + at:5 + at, :] = jnp.broadcast_to(ROOT_DT * (field - xr), (1, LANES))
        msgs[0, me, 8 + i:9 + i, :] = jnp.broadcast_to(log_part, (1, LANES))

    spread_wait(counts_run, 0)
    spread_start(counts_run, 1)

    def m_copy(k, owner, target):
        return remote(msgs.at[0, owner], msgs.at[0, owner], m_send.at[k], m_recv.at[k], {"chol": target})

    @pl.loop(1, nchol)
    def _(k):
        m_copy(k, me, lax.rem(me + k, nchol)).start()

    @pl.loop(1, nchol)
    def _(k):
        owner = lax.rem(me + nchol - k, nchol)
        l_copy(k, owner, owner).wait_recv()
        z_copy(k, owner, parity).start()
        f_copy(k, owner, core, parity, 0).start()

    @pl.loop(1, nchol)
    def _(k):
        owner = lax.rem(me + nchol - k, nchol)
        m_copy(k, owner, owner).wait_recv()

    cols = pl.multiple_of(mine_half * first, 8)

    def n_copy(j, shift):
        return remote(msgs.at[0, :, pl.ds(0, 8)], msgs.at[j + 1, :, pl.ds(0, 8)], n_send.at[j], n_recv.at[j], walk_id(shift))

    def p_copy(j, shift):
        return remote(padt.at[:, :, pl.ds(cols, quarter)], pcand.at[j], n_send.at[2 + j], n_recv.at[2 + j], walk_id(shift))

    n_copy(0, 1).start()
    n_copy(1, -1).start()
    spread_wait(counts_run, 1)
    spread_start(counts_run, 2)

    @pl.loop(1, nchol)
    def _(k):
        owner = lax.rem(me + nchol - k, nchol)
        z_copy(k, owner, 1 - parity).wait_recv()
        f_copy(k, owner, core, 1 - parity, 1).start()

    p_copy(0, 1).start()
    p_copy(1, -1).start()

    for i in range(walks):
        log_weight = msgs[0, 0, 8 + i:9 + i, :]
        for o in range(1, nchol):
            log_weight = log_weight + msgs[0, o, 8 + i:9 + i, :]
        ring[here, core, i:i + 1, :] = weights_s[i] * jnp.exp(log_weight)

    spread_start(weights_run, 0)

    @pl.loop(1, nchol)
    def _(k):
        owner = lax.rem(me + nchol - k, nchol)
        f_copy(k, owner, 1 - core, parity, 0).wait_recv()
        f_copy(k, owner, 1 - core, 1 - parity, 1).wait_recv()

    spread_wait(counts_run, 2)
    zero = jnp.zeros((1, LANES), F32)
    base_count = zero
    for d in range(-here, here):
        if d == 0:
            earlier = [core == 1, core < 0]
        elif d < 0:
            earlier = [chip + d >= 0] * 2
        else:
            earlier = [chip + d >= nchip] * 2
        for c in range(2):
            base_count = base_count + jnp.where(
                earlier[c], tally[here + d, c, 0:1, :] + tally[here + d, c, 1:2, :], 0.0)
    def counts_of(when_even, when_odd, i):
        return jnp.where(core == 0, tally[when_even[0], when_even[1], i:i + 1, :],
                         tally[when_odd[0], when_odd[1], i:i + 1, :])

    own_counts = [tally[here, core, i:i + 1, :] for i in range(walks)]
    left_counts = [counts_of((here - 1, 1), (here, 0), i) for i in range(walks)]
    right_counts = [counts_of((here, 1), (here + 1, 0), i) for i in range(walks)]
    left_start = base_count - left_counts[0] - left_counts[1]
    right_start = base_count + own_counts[0] + own_counts[1]
    weights_of = []
    for start, cs, valid in (
        (base_count, own_counts, w >= 0),
        (left_start, left_counts, w > 0),
        (right_start, right_counts, w < nwalk - 1),
    ):
        for i in range(walks):
            end = start + cs[i]
            picks = []
            for m in range(walks):
                target = jnp.full((1, LANES), (w * walks + m).astype(F32))
                hit = jnp.where(start <= target, 1.0, 0.0) * jnp.where(target < end, 1.0, 0.0)
                picks.append(jnp.where(valid, hit, 0.0))
            weights_of.append(picks)
            start = end
    n_copy(0, 1).wait_recv()
    n_copy(1, -1).wait_recv()
    for ri in range(2):
        for m in range(walks):
            for g in range(2):
                acc = jnp.zeros((nchol, LANES), F32)
                for j in range(3 * walks):
                    acc = acc + weights_of[j][m] * msgs[j // walks, :, 4 * ri + 2 * (j % walks) + g, :]
                cnew[4 * ri + 2 * m + g] = acc

    copy_own.wait()

    part = rows // 2
    pieces = []
    for h in range(2):
        sums = [jnp.zeros((part, norb), F32) for _ in range(4)]
        for o in range(nchol):
            for g in range(2):
                l = lrows[o, g, h * part:(h + 1) * part, :]
                for i in range(walks):
                    for ri in range(2):
                        at = 4 * ri + 2 * i + g
                        c = jnp.concatenate([cnew[at, o:o + 1, :]] * (norb // LANES), axis=1)
                        sums[2 * i + ri] = sums[2 * i + ri] + c * l
        pieces.append(sums)
    for i in range(walks):
        for ri in range(2):
            for h in range(2):
                acomp[i, ri, h * part:(h + 1) * part, :] = pieces[h][2 * i + ri]

    def band_rows(by):
        return pl.ds(pl.multiple_of(by * rows, rows), rows)

    def a_copy(d):
        to = lax.rem(gy + d, side)
        return remote(acomp.at[lax.div(to, 2)], abuf.at[:, band_rows(gy)], a_send.at[d], a_recv.at[d],
                      {"chol": chip_at(0, d)})

    for d in (2, 1, 3):
        a_copy(d).start()
    abuf[:, band_rows(gy), :] = acomp[mine_walker]
    p_copy(0, 1).wait_recv()
    p_copy(1, -1).wait_recv()
    picked = jnp.zeros((2, quarter, norb), F32)
    for j in range(3 * walks):
        i = j % walks
        source = padt[i, :, pl.ds(cols, quarter), :] if j < walks else pcand[j // walks - 1, i]
        pick = jnp.where(mine_walker == 0, weights_of[j][0], weights_of[j][1])
        picked = picked + jnp.concatenate([pick] * (norb // LANES), axis=1)[None] * source
    q0[...] = picked.reshape(2 * quarter, norb).T
    spread_wait(weights_run, 0)
    spread_start(weights_run, 1)
    q_split = split(q0[...])
    minus = jnp.where(lax.broadcasted_iota(jnp.int32, (band, LANES), 1) < quarter, -1.0, 1.0).astype(F32)

    def apply(oper, values, depth_of):
        prod = dot3(oper, values)
        return prod[:depth_of] + minus[:depth_of] * pltpu.roll(prod[depth_of:], quarter, 1)

    def strip(by):
        return pl.ds(pl.multiple_of(gx * band + by * rows, rows), rows)

    def s_copy(e, d):
        ref = q1.at[strip(lax.rem(gy + side - e, side))]
        return remote(ref, ref, s_send.at[e, d], s_recv.at[e, d], {"chol": chip_at(d, 0)})

    for e in (0, 1, 3, 2):
        by = lax.rem(gy + side - e, side)
        if e:
            a_copy(e).wait_recv()
        q1[strip(by), :] = apply(split(abuf[:, band_rows(by), :].reshape(2 * rows, norb)), q_split, rows)
        for d in (2, 1, 3):
            s_copy(e, d).start()
    oper = split(abuf[...].reshape(2 * band, norb))

    def g_copy(n, q, d):
        ref = q.at[at_band(gx)]
        return remote(ref, ref, g_send.at[n, d], g_recv.at[n, d], {"chol": chip_at(d, 0)})

    series = q0[at_band(gx), :] + q1[at_band(gx), :]
    spread_wait(weights_run, 1)
    spread_start(weights_run, 2)
    for n in range(2, TAYLOR + 1):
        if n == 2:
            for e in (0, 1, 3, 2):
                for d in (1, 3, 2):
                    s_copy(e, d).wait_recv()
            term = apply(oper, split(q1[...]), band) / n
            q2[at_band(gx), :] = term
            for d in (2, 1, 3):
                g_copy(1, q2, d).start()
        else:
            for d in (1, 3, 2):
                g_copy(1, q2, d).wait_recv()
            term = apply(oper, split(q2[...]), band) / n
        series = series + term
    turned = series.T
    for c in range(2):
        qf[gy, c, :, at_band(gx)] = turned[c * quarter:c * quarter + first]

    def o_copy(c, sem, origin, to):
        (da, db), (ta, tb) = origin, to
        dx, dy = (da, db) if c == 0 else (db, da)
        tx, ty = (ta, tb) if c == 0 else (tb, ta)
        ref = qf.at[lax.rem(gy + side + dy, side), c, :,
                    pl.ds(pl.multiple_of(lax.rem(gx + side + dx, side) * band, band), band)]
        return remote(ref, ref, o_send.at[c, sem], o_recv.at[c, sem], {"chol": chip_at(tx, ty)})

    def o_send_first(c, d):
        return o_copy(c, d, (0, 0), (d, 0))

    def o_send_second(c, d, e):
        return o_copy(c, 4 * d + e, (-d, 0), (0, e)) if d else o_copy(c, 16 + e, (0, 0), (0, e))

    def o_recv_first(c, d):
        return o_copy(c, d, (-d, 0), (d, 0))

    def o_recv_second(c, d, e):
        return o_copy(c, 4 * d + e, (-d, -e), (0, e)) if d else o_copy(c, 16 + e, (0, -e), (0, e))

    for d in (2, 1, 3):
        for c in range(2):
            o_send_first(c, d).start()
    for d in (2, 1, 3):
        for c in range(2):
            o_send_second(c, 0, d).start()
    spread_wait(weights_run, 2)
    zero = jnp.zeros((1, LANES), F32)
    total, base = zero, zero
    for d in range(-here, here):
        if d == 0:
            earlier = [core == 1, core < 0]
        elif d < 0:
            earlier = [chip + d >= 0] * 2
        else:
            earlier = [chip + d >= nchip] * 2
        for c in range(2):
            pair = ring[here + d, c, 0:1, :] + ring[here + d, c, 1:2, :]
            total = total + pair
            base = base + jnp.where(earlier[c], pair, 0.0)
    running = base
    for i in range(walks):
        running = running + ring[here, core, i:i + 1, :]
        comb_s[i] = jnp.max(nwalk * walks * running / total)

    for d in (1, 3, 2):
        for c in range(2):
            o_recv_first(c, d).wait_recv()
            for e in (2, 1, 3):
                o_send_second(c, d, e).start()
    for c in range(2):
        for d in (0, 1, 3, 2):
            for e in (1, 3, 2):
                o_recv_second(c, d, e).wait_recv()
    rest = nelec - first
    for i in range(walks):
        for c in range(2):
            wbuf[i, c * nelec:c * nelec + first, :] = qf[2 * i, c]
            wbuf[i, c * nelec + first:(c + 1) * nelec, :] = qf[2 * i + 1, c, 0:rest, :]
        pltpu.make_async_copy(wbuf.at[i], out_ref.at[i], c_sem.at[3 + i]).start()

    @pl.loop(1, nchol)
    def _(k):
        owner = lax.rem(me + nchol - k, nchol)
        l_copy(k, owner, owner).wait_send()
        z_copy(k, owner, parity).wait_send()
        f_copy(k, owner, core, parity, 0).wait_send()
        f_copy(k, owner, core, 1 - parity, 1).wait_send()
        m_copy(k, owner, owner).wait_send()

    for copy in (n_copy, p_copy):
        copy(0, 1).wait_send()
        copy(1, -1).wait_send()
    for d in range(1, side):
        a_copy(d).wait_send()
        for e in range(side):
            s_copy(e, d).wait_send()
        g_copy(1, q2, d).wait_send()
        for c in range(2):
            o_send_first(c, d).wait_send()
            for e in range(side):
                o_send_second(c, e, d).wait_send()
    for i in range(walks):
        pltpu.make_async_copy(wbuf.at[i], out_ref.at[i], c_sem.at[3 + i]).wait()


def solution(mesh):
    nwalk, nchol = mesh.shape["walk"], mesh.shape["chol"]

    def on_device(walkers, cholesky, fields, weights, counts):
        walks, norb, width = walkers.shape
        nelec = width // 2
        ng = cholesky.shape[0]
        rows = norb // nchol
        depth = -(-nelec // 8) * 8
        vmem = pltpu.VMEM
        dma = pltpu.SemaphoreType.DMA
        smem = pl.BlockSpec(memory_space=pltpu.SMEM)
        hbm = pl.BlockSpec(memory_space=pl.ANY)
        routed, comb = pl.pallas_call(
            functools.partial(kernel, nwalk, nchol, nelec),
            out_shape=(
                jax.ShapeDtypeStruct((walks, width, norb), F32),
                jax.ShapeDtypeStruct((walks,), F32),
            ),
            in_specs=[hbm, hbm, smem, smem, smem],
            out_specs=(hbm, smem),
            scratch_shapes=[
                vmem((walks, width, norb), F32),
                vmem((walks, 2, LANES, norb), F32),
                vmem((ng, depth, norb), F32),
                vmem((nchol, ng, rows, norb), F32),
                vmem((walks, norb, 2 * LANES), F32),
                vmem((walks, norb, 2 * LANES), BF16),
                vmem((walks, norb, 2 * LANES), BF16),
                vmem((3, nchol, 16, LANES), F32),
                vmem((walks, 2, rows, norb), F32),
                vmem((2, 4 * rows, norb), F32),
                vmem((norb, LANES), F32),
                vmem((norb, LANES), F32),
                vmem((norb, LANES), F32),
                vmem((8, nchol, LANES), F32),
                vmem((2, walks, 2, LANES // 2, norb), F32),
                vmem((4, 2, -(-nelec // 16) * 8, norb), F32),
                vmem((nwalk // 2, 2, 8, LANES), F32),
                vmem((nwalk // 2, 2, 8, LANES), F32),
                dma((5,)),
                dma((nchol,)), dma((nchol,)), dma((nchol,)), dma((nchol,)),
                dma((2, nchol)), dma((2, nchol)), dma((nchol,)), dma((nchol,)),
                dma((4,)), dma((4,)), dma((4, 4)), dma((4, 4)), dma((2, 4)), dma((2, 4)), dma((2, 20)), dma((2, 20)),
                dma((9,)), dma((9,)), dma((9,)), dma((9,)),
                dma((4,)), dma((4,)),
            ],
            compiler_params=pltpu.CompilerParams(collective_id=0, has_side_effects=True),
        )(jnp.swapaxes(walkers, 1, 2), cholesky, fields, weights, counts)
        return jnp.swapaxes(routed, 1, 2), comb

    in_specs = (P("walk", None, None), P("chol", None, None), P("walk", "chol"), P("walk"), P("walk"))
    return jax.shard_map(
        on_device, mesh=mesh, in_specs=in_specs, out_specs=(P("walk", None, None), P("walk")), check_vma=False
    )
```

time: 73.8 us -> 70.1 us (0.950)
  the two profiles are of different devices: /device:TPU:1 before, /device:TPU:8 now
where the time goes in v3:
time: 70.1 us; the launch traced here: 69.9 us
  Pallas kernels  66 us (94%)
  local copies, waits for them, and re-layouts  3.26 us (5%)
    pallas_call x1, Pallas kernels, on_device(): pl.pallas_call(functools.partial(kernel, nwalk, nchol, nelec), out_shape=...  66 us
    unnamed x2, local copies, waits for them, and re-layouts  3.26 us

profile of v3, /device:TPU:8, one launch (start us, length us, event | category | flops | bytes accessed | tf_op | source)
XLA Modules:
  0.0 69.9 jit_solution(4156247881461861255)
XLA Ops:
  0.6 66.0 %shard_map.68 = (f32[2,200,512]{2,1,0:T(8,128)}, f32[2]{0:T(128)}) custom-call(f32[2,200,512]{2,1,0:T(8,128)} %bitcast.2, f32[2,512,512]{2,1,0:T(8,128)} %chol_hbm.1, f32[2,2]{1,0:T(2,128)} %fields_s.1, f32[2]{0:T(128)} %weights_s.1, s32[2]{0:T(128)} %counts_s.1), custom_call_target="tpu_custom_call" | custom-call | tf_op jit(solution)/shard_map/pallas_call | solution.py:498
  66.7 2.1 %copy.9 = f32[2,512,200]{1,2,0:T(8,128)} copy(f32[2,512,200]{1,2,0:T(8,128)} %bitcast.3) | data formatting | bytes 1638400
  68.8 1.2 %copy.10 = f32[2]{0:T(128)} copy(f32[2]{0:T(128)} %get-tuple-element.9) | data formatting | bytes 16

commit v4 on v3

--- a/solution.py
+++ b/solution.py
@@ -480,6 +480,12 @@
                 o_send_second(c, e, d).wait_send()
     for i in range(walks):
         pltpu.make_async_copy(wbuf.at[i], out_ref.at[i], c_sem.at[3 + i]).wait()
+
+
+def hand_over(values, marks, values_out, marks_out):
+    values_out[...] = values[...]
+    for i in range(marks.shape[0]):
+        marks_out[i] = marks[i]
 
 
 def solution(mesh):
@@ -531,6 +537,13 @@
             ],
             compiler_params=pltpu.CompilerParams(collective_id=0, has_side_effects=True),
         )(jnp.swapaxes(walkers, 1, 2), cholesky, fields, weights, counts)
+        whole = pl.BlockSpec(memory_space=pltpu.VMEM)
+        routed, comb = pl.pallas_call(
+            hand_over,
+            out_shape=(jax.ShapeDtypeStruct(routed.shape, F32), jax.ShapeDtypeStruct(comb.shape, F32)),
+            in_specs=[whole, smem],
+            out_specs=(whole, smem),
+        )(routed, comb)
         return jnp.swapaxes(routed, 1, 2), comb
 
     in_specs = (P("walk", None, None), P("chol", None, None), P("walk", "chol"), P("walk"), P("walk"))

time: 70.1 us -> 68.9 us (0.983)
  local copies, waits for them, and re-layouts: 3.26 us -> 0 us
  Pallas kernels: 66 us -> 68.1 us
    unnamed x2 -> x0, local copies, waits for them, and re-layouts: 3.26 us -> none
    pallas_call x0 -> x1, Pallas kernels: none -> 2.11 us  [on_device(): pl.pallas_call(hand_over, out_shape=(jax.ShapeDtypeStruct(routed.shape, F...]
where the time goes in v4:
time: 68.9 us; the launch traced here: 68.8 us
  Pallas kernels  68.1 us (99%)
    pallas_call x1, Pallas kernels, on_device(): pl.pallas_call(functools.partial(kernel, nwalk, nchol, nelec), out_shape=...  66 us
    pallas_call x1, Pallas kernels, on_device(): pl.pallas_call(hand_over, out_shape=(jax.ShapeDtypeStruct(routed.shape, F...  2.11 us

profile of v4, /device:TPU:8, one launch (start us, length us, event | category | flops | bytes accessed | tf_op | source)
XLA Modules:
  0.0 68.8 jit_solution(222960185201623281)
XLA Ops:
  0.6 66.0 %shard_map.68 = (f32[2,200,512]{2,1,0:T(8,128)}, f32[2]{0:T(128)}) custom-call(f32[2,200,512]{2,1,0:T(8,128)} %bitcast.2, f32[2,512,512]{2,1,0:T(8,128)} %chol_hbm.1, f32[2,2]{1,0:T(2,128)} %fields_s.1, f32[2]{0:T(128)} %weights_s.1, s32[2]{0:T(128)} %counts_s.1), custom_call_target="tpu_custom_call" | custom-call | tf_op jit(solution)/shard_map/pallas_call | solution.py:504
  66.7 2.1 %shard_map.69 = (f32[2,200,512]{2,1,0:T(8,128)}, f32[2]{0:T(128)}) custom-call(f32[2,200,512]{2,1,0:T(8,128)} %get-tuple-element.6.values, f32[2]{0:T(128)} %get-tuple-element.7.marks), custom_call_target="tpu_custom_call" | custom-call | tf_op jit(solution)/shard_map/pallas_call | solution.py:541
